TPU v7x, 32 devices: a whole 2x2x4 slice. The times are simulated.
32 devices in a mesh: seq: 8 (over y, x, core), req: 4 (over z).
Axes of the slice: x: 2, y: 2, z: 4, core: 2. Of those that a mesh axis runs over, the one named last changes fastest.
Arguments:
- queries: bfloat16 [8, 256, 1536], P('req', 'seq'), as said below
- new_kv: bfloat16 [2, 8, 256, 512], P(None, 'req', 'seq'), may hold values from -6 to 6
- cache_kv: bfloat16 [2, 8, 2048, 512], P(None, 'req', 'seq'), as said below
- cache_spans: int32 [8, 2], P('req'), may hold values from 0 to 2048, as said below
- recompute_rows: int32 [8, 256], P('req'), may hold values from 0 to 2047, as said below
- held_states: bfloat16 [8, 256, 1536], P('req', 'seq'), may hold values from -6 to 6
- key_weight: bfloat16 [1536, 512], replicated, may hold values from -0.15625 to 0.15625
- norm_gain: float32 [1536], replicated, may hold values from 0.1 to 1.9
- routes: int32 [8, 256, 8], P('req', 'seq'), may hold values from 0 to 19, all different within a row; in each aligned block of 32 rows (0 to 31, 32 to 63, ..., all dimensions but the last counted through in order) at most 16 rows name the same one
- route_weights: float32 [8, 256, 8], P('req', 'seq'), may hold values from 0.05 to 1
- expert_gate_up: bfloat16 [20, 1536, 1024], P('req'), may hold values from -0.15625 to 0.15625
- expert_down: bfloat16 [20, 512, 1536], P('req'), may hold values from -0.25 to 0.25
Outputs:
- layer_out: bfloat16 [8, 256, 1536], P('req', 'seq')
Inputs may be any that keep to these rules, and one draw needn't show every extreme that they name: `routes`: in each aligned block of 32 rows of one request (one device's rows of that request) no expert is named more than 16 times. cache_spans[r] = (start, length): 1024 <= length <= 2048 with some request of length 2048; 0 <= start <= 512 with some request starting at 0. `recompute_rows`: within a request the rows are distinct and lie between the request's start and length. `queries`: entries lie within -6 to 6. `cache_kv`: entries lie within -6 to 6.
All inputs are finite; a program needn't handle non-finite values.
Results may differ from a plain program's by a relative error of at most 0.034.
Values may be sent and summed in bfloat16 or wider, within the bound.
A program may use at most 192 MiB of HBM per device.

v0:
```python
import jax
import jax.numpy as jnp
from jax import lax
from jax.sharding import PartitionSpec as P

H = 24
KVH = 8
HD = 64
FF = 512
TOP = 8
CAP = 16
NEG = -1e30
THETA = 10000.0


def rotate(key_heads, positions):
    half_dim = key_heads.shape[-1] // 2
    exponent = jnp.arange(half_dim).astype(jnp.float32) * (2.0 / key_heads.shape[-1])
    inverse = THETA ** (-exponent)
    angles = positions.astype(jnp.float32)[..., None] * inverse
    cosine = jnp.cos(angles)[..., None, :]
    sine_part = jnp.sin(angles)[..., None, :]
    lower_half = key_heads[..., :half_dim]
    upper_half = key_heads[..., half_dim:]
    return jnp.concatenate(
        [
            lower_half * cosine - upper_half * sine_part,
            upper_half * cosine + lower_half * sine_part,
        ],
        axis=-1,
    )


def partial_attend(packed):
    query_rows, key_rows, value_rows, allowed = packed
    query_count, model_width = query_rows.shape
    key_count = key_rows.shape[0]
    groups = H // KVH
    query_heads = query_rows.reshape(query_count, KVH, groups, HD)
    key_heads = key_rows.reshape(key_count, KVH, HD)
    value_heads = value_rows.reshape(key_count, KVH, HD)
    scores = jnp.einsum(
        "qkgd,nkd->kgqn", query_heads, key_heads, preferred_element_type=jnp.float32
    ) * HD ** (-0.5)
    scores = jnp.where(allowed[None, None, :, :], scores, NEG)
    highest = jnp.max(scores, axis=-1, keepdims=True)
    exps = jnp.exp(scores - highest)
    totals = jnp.sum(exps, axis=-1)
    weights = exps.astype(jnp.bfloat16)
    mixed_rows = jnp.einsum(
        "kgqn,nkd->qkgd", weights, value_heads, preferred_element_type=jnp.float32
    )
    mixed_rows = mixed_rows / jnp.transpose(totals, (2, 0, 1))[..., None]
    log_total = highest[..., 0] + jnp.log(totals)
    log_rows = jnp.transpose(log_total, (2, 0, 1)).reshape(query_count, H)
    return (mixed_rows.reshape(query_count, model_width), log_rows)


def body_wide(
    queries,
    new_kv,
    cache_kv,
    cache_spans,
    recompute_rows,
    held_states,
    key_weight,
    norm_gain,
    routes,
    route_weights,
    expert_gate_up,
    expert_down,
):
    seq_index = lax.axis_index("seq")
    seq_count = lax.axis_size("seq")
    owner_count = lax.axis_size("req")
    req_rows, tok_rows, model_width = queries.shape
    cache_rows = cache_kv.shape[2]
    held_rows = held_states.shape[1]
    local_experts = expert_gate_up.shape[0]
    expert_total = owner_count * local_experts
    my_positions = lax.dynamic_slice_in_dim(recompute_rows, seq_index * held_rows, held_rows, 1)
    projected = jnp.dot(
        held_states.reshape(req_rows * held_rows, model_width),
        key_weight,
        preferred_element_type=jnp.float32,
    )
    rotated = rotate(projected.reshape(req_rows, held_rows, KVH, HD), my_positions)
    rotated = rotated.reshape(req_rows, held_rows, KVH * HD).astype(jnp.bfloat16)
    fresh_rows = lax.all_gather(rotated, "seq", axis=1, tiled=True)
    cache_positions = seq_index * cache_rows + jnp.arange(cache_rows)
    hit_table = recompute_rows[:, None, :] == cache_positions[None, :, None]
    placed = jnp.einsum(
        "rcm,rmk->rck",
        hit_table.astype(jnp.bfloat16),
        fresh_rows,
        preferred_element_type=jnp.float32,
    ).astype(jnp.bfloat16)
    cache_keys = jnp.where(jnp.any(hit_table, axis=2)[:, :, None], placed, cache_kv[0])
    span_start = cache_spans[:, 0:1]
    span_end = cache_spans[:, 1:2]
    all_queries = lax.all_gather(queries, "seq", axis=1, tiled=True)
    step_total = all_queries.shape[1]
    cache_allowed = (cache_positions[None, :] >= span_start) & (cache_positions[None, :] < span_end)
    key_positions = seq_index * tok_rows + jnp.arange(tok_rows)
    step_allowed = key_positions[None, :] <= jnp.arange(step_total)[:, None]
    allowed = jnp.concatenate(
        [
            jnp.broadcast_to(cache_allowed[:, None, :], (req_rows, step_total, cache_rows)),
            jnp.broadcast_to(step_allowed[None], (req_rows, step_total, tok_rows)),
        ],
        axis=2,
    )
    key_rows = jnp.concatenate([cache_keys, new_kv[0]], axis=1)
    value_rows = jnp.concatenate([cache_kv[1], new_kv[1]], axis=1)
    part_out, part_log = lax.map(partial_attend, (all_queries, key_rows, value_rows, allowed))
    piece_out, piece_log = (
        lax.all_to_all(part_out[None], "seq", split_axis=2, concat_axis=0, tiled=True),
        lax.all_to_all(part_log[None], "seq", split_axis=2, concat_axis=0, tiled=True),
    )
    best_log = jnp.max(piece_log, axis=0)
    factors = jnp.exp(piece_log - best_log[None])
    factor_sum = jnp.sum(factors, axis=0)
    spread_out = piece_out.reshape(seq_count, req_rows, tok_rows, H, HD)
    combined = jnp.sum(spread_out * factors[..., None], axis=0) / factor_sum[..., None]
    attended_f = combined.reshape(req_rows, tok_rows, model_width)
    attended = attended_f.astype(jnp.bfloat16)
    attended_f = attended.astype(jnp.float32)
    mean_square = jnp.mean(attended_f * attended_f, axis=-1, keepdims=True)
    normed = (attended_f * lax.rsqrt(mean_square + 1e-06) * norm_gain).astype(jnp.bfloat16)
    route_flat = routes.reshape(req_rows, tok_rows * TOP)
    expert_match = (route_flat[:, :, None] == jnp.arange(expert_total)[None, None, :]).astype(
        jnp.int32
    )
    earlier = jnp.cumsum(expert_match, axis=1) - expert_match
    slot_index = jnp.sum(earlier * expert_match, axis=2)
    target = route_flat * CAP + slot_index
    slot_match = target[:, :, None] == jnp.arange(expert_total * CAP)[None, None, :]
    dispatch = jnp.any(
        slot_match.reshape(req_rows, tok_rows, TOP, expert_total * CAP), axis=2
    ).astype(jnp.bfloat16)
    dispatch = dispatch.reshape(req_rows, tok_rows, owner_count, local_experts, CAP)
    outgoing = jnp.einsum(
        "rtnec,rtd->nrecd", dispatch, normed, preferred_element_type=jnp.float32
    ).astype(jnp.bfloat16)
    hidden = jnp.einsum(
        "srecd,edf->srecf",
        lax.all_to_all(outgoing, "req", split_axis=0, concat_axis=0, tiled=True),
        expert_gate_up,
        preferred_element_type=jnp.float32,
    )
    active = (jax.nn.silu(hidden[..., :FF]) * hidden[..., FF:]).astype(jnp.bfloat16)
    result = jnp.einsum(
        "srecf,efd->srecd", active, expert_down, preferred_element_type=jnp.float32
    ).astype(jnp.bfloat16)
    returned = lax.all_to_all(result, "req", split_axis=0, concat_axis=0, tiled=True)
    owner_of = route_flat // local_experts
    local_of = route_flat % local_experts
    flat_index = (
        (owner_of * req_rows + jnp.arange(req_rows)[:, None]) * local_experts + local_of
    ) * CAP + slot_index
    returned_rows = jnp.take(returned.reshape(-1, model_width), flat_index.reshape(-1), axis=0)
    returned_rows = returned_rows.reshape(req_rows, tok_rows, TOP, model_width)
    mixture = jnp.einsum(
        "rtk,rtkd->rtd",
        route_weights,
        returned_rows.astype(jnp.float32),
        precision=lax.Precision.HIGHEST,
    )
    return (attended_f + mixture).astype(jnp.bfloat16)


def head_parallel_body(
    queries,
    new_kv,
    cache_kv,
    cache_spans,
    recompute_rows,
    held_states,
    key_weight,
    norm_gain,
    routes,
    route_weights,
    expert_gate_up,
    expert_down,
):
    seq_index = lax.axis_index("seq")
    seq_count = lax.axis_size("seq")
    req_index = lax.axis_index("req")
    owner_count = lax.axis_size("req")
    req_rows, tok_rows, model_width = queries.shape
    cache_rows = cache_kv.shape[2]
    held_rows = held_states.shape[1]
    local_experts = expert_gate_up.shape[0]
    groups = H // KVH
    bf16 = jnp.bfloat16
    f32 = jnp.float32
    my_positions = lax.dynamic_slice_in_dim(recompute_rows, seq_index * held_rows, held_rows, 1)
    projected = jnp.dot(
        held_states.reshape(req_rows * held_rows, model_width),
        key_weight,
        preferred_element_type=f32,
    )
    rotated = rotate(projected.reshape(req_rows, held_rows, KVH, HD), my_positions).astype(bf16)
    kv = jnp.concatenate([cache_kv, new_kv], axis=2)
    kv = kv.reshape(2, req_rows, cache_rows + tok_rows, KVH, HD).transpose(3, 1, 2, 0, 4)
    kv = kv.reshape(KVH, req_rows, cache_rows + tok_rows, 2 * HD)
    kv = lax.all_to_all(kv, "seq", split_axis=0, concat_axis=0, tiled=True)
    query_pack = queries.reshape(req_rows, tok_rows, KVH, groups * HD).transpose(2, 0, 1, 3)
    query_pack = lax.all_to_all(query_pack, "seq", split_axis=0, concat_axis=0, tiled=True)
    fresh = lax.all_to_all(
        rotated.transpose(2, 0, 1, 3), "seq", split_axis=0, concat_axis=0, tiled=True
    )
    fresh = fresh.transpose(1, 0, 2, 3).reshape(req_rows, seq_count * held_rows, HD)
    cache_total = seq_count * cache_rows
    step_total = seq_count * tok_rows
    cache_part = kv[:, :, :cache_rows].transpose(1, 0, 2, 3).reshape(req_rows, cache_total, 2 * HD)
    step_part = kv[:, :, cache_rows:].transpose(1, 0, 2, 3).reshape(req_rows, step_total, 2 * HD)
    positions = jnp.arange(cache_total)
    hit_table = recompute_rows[:, None, :] == positions[None, :, None]
    placed = jnp.einsum(
        "rcm,rmk->rck", hit_table.astype(bf16), fresh, preferred_element_type=f32
    ).astype(bf16)
    cache_keys = jnp.where(jnp.any(hit_table, axis=2)[:, :, None], placed, cache_part[..., :HD])
    keys = jnp.concatenate([cache_keys, step_part[..., :HD]], axis=1)
    values = jnp.concatenate([cache_part[..., HD:], step_part[..., HD:]], axis=1)
    heads = query_pack.reshape(seq_count, req_rows, tok_rows, groups, HD).transpose(1, 3, 0, 2, 4)
    heads = heads.reshape(req_rows, groups, step_total, HD)
    scores = jnp.einsum("rgqd,rnd->rgqn", heads, keys, preferred_element_type=f32) * HD ** (-0.5)
    cache_allowed = (positions[None] >= cache_spans[:, 0:1]) & (
        positions[None] < cache_spans[:, 1:2]
    )
    step_allowed = jnp.arange(step_total)[None, :] <= jnp.arange(step_total)[:, None]
    allowed = jnp.concatenate(
        [
            jnp.broadcast_to(cache_allowed[:, None, :], (req_rows, step_total, cache_total)),
            jnp.broadcast_to(step_allowed[None], (req_rows, step_total, step_total)),
        ],
        axis=2,
    )
    scores = jnp.where(allowed[:, None], scores, NEG)
    exps = jnp.exp(scores - jnp.max(scores, axis=-1, keepdims=True))
    totals = jnp.sum(exps, axis=-1, keepdims=True)
    mixed = jnp.einsum("rgqn,rnd->rgqd", exps.astype(bf16), values, preferred_element_type=f32)
    mixed = (mixed / totals).astype(bf16)
    mixed = mixed.reshape(req_rows, groups, seq_count, tok_rows, HD).transpose(2, 0, 3, 1, 4)
    mixed = mixed.reshape(seq_count, req_rows, tok_rows, groups * HD)
    mixed = lax.all_to_all(mixed, "seq", split_axis=0, concat_axis=0, tiled=True)
    attended = mixed.transpose(1, 2, 0, 3).reshape(req_rows * tok_rows, model_width)
    attended_f = attended.astype(f32)
    mean_square = jnp.mean(attended_f * attended_f, axis=-1, keepdims=True)
    normed = (attended_f * lax.rsqrt(mean_square + 1e-06) * norm_gain).astype(bf16)
    tokens = lax.all_gather(normed, "req", axis=0, tiled=True)
    all_routes = lax.all_gather(routes.reshape(req_rows * tok_rows, TOP), "req", axis=0, tiled=True)
    all_weights = lax.all_gather(
        route_weights.reshape(req_rows * tok_rows, TOP), "req", axis=0, tiled=True
    )
    mine = req_index * local_experts + jnp.arange(local_experts)
    share = jnp.sum(
        jnp.where(all_routes[:, :, None] == mine[None, None], all_weights[:, :, None], 0.0), axis=1
    )
    total = jnp.zeros(tokens.shape, f32)
    for e in range(local_experts):
        hidden = jnp.dot(tokens, expert_gate_up[e], preferred_element_type=f32)
        active = (jax.nn.silu(hidden[:, :FF]) * hidden[:, FF:]).astype(bf16)
        result = jnp.dot(active, expert_down[e], preferred_element_type=f32).astype(bf16)
        total = total + result.astype(f32) * share[:, e : e + 1]
    pieces = total.astype(bf16).reshape(owner_count, req_rows * tok_rows, model_width)
    pieces = lax.all_to_all(pieces, "req", split_axis=0, concat_axis=0, tiled=True)
    mixture = jnp.sum(pieces.astype(f32), axis=0)
    return (attended_f + mixture).astype(bf16).reshape(req_rows, tok_rows, model_width)


def solution(mesh):
    body = head_parallel_body if mesh.shape["seq"] == KVH else body_wide
    in_specs = (
        P("req", "seq", None),
        P(None, "req", "seq", None),
        P(None, "req", "seq", None),
        P("req", None),
        P("req", None),
        P("req", "seq", None),
        P(),
        P(),
        P("req", "seq", None),
        P("req", "seq", None),
        P("req", None, None),
        P("req", None, None),
    )
    out_specs = P("req", "seq", None)
    return jax.shard_map(body, mesh=mesh, in_specs=in_specs, out_specs=out_specs, check_vma=False)
```

profile of v0, /device:TPU:0, one launch (start us, length us, event | category | flops | bytes accessed | tf_op | source)
XLA Modules:
  0.0 173.9 jit_solution(13547308417040345744)
XLA Ops:
  0.0 1.8 %copy.124 = bf16[1536,512]{0,1:T(8,128)(2,1)S(1)} copy(bf16[1536,512]{1,0:T(8,128)(2,1)} %param.18) | data formatting | bytes 3145728 | tf_op args[6]
  4.1 5.2 %all-to-all-start = ((bf16[8,2,2048]{2,1,0:T(2,128)(2,1)}), bf16[8,2,2048]{2,1,0:T(2,128)(2,1)S(1)}, u32[]{:S(2)}, u32[]{:S(2)}) async-start(bf16[8,2,2048]{2,1,0:T(2,128)(2,1)} %reshape.168), calls=%async_computation | async-start | bytes 131072 | tf_op jit(solution)/shard_map/all_to_all | solution.py:210
  9.4 13.3 %all-gather.1 = f32[4,64,8]{1,2,0:T(8,128)S(1)} all-gather(f32[1,64,8]{1,2,0:T(8,128)S(1)} %reshape.158), channel_id=1, replica_groups=mesh['seq'=8,'req'=4] {'req'}, dimensions={0}, use_global_device_ids=true | all-gather | bytes 10240 | tf_op jit(solution)/shard_map/all_gather | solution.py:254
  22.9 13.1 %all-gather = s32[4,64,8]{1,2,0:T(8,128)S(1)} all-gather(s32[1,64,8]{1,2,0:T(8,128)S(1)} %reshape.156), channel_id=1, replica_groups=mesh['seq'=8,'req'=4] {'req'}, dimensions={0}, use_global_device_ids=true | all-gather | bytes 10240 | tf_op jit(solution)/shard_map/all_gather | solution.py:253
  38.3 1.6 copy.131
  39.9 4.2 %all-to-all-start.2 = ((bf16[8,2,32,192]{3,2,1,0:T(8,128)(2,1)}), bf16[8,2,32,192]{3,2,1,0:T(8,128)(2,1)S(1)}, u32[]{:S(2)}, u32[]{:S(2)}) async-start(bf16[8,2,32,192]{3,2,1,0:T(8,128)(2,1)} %bitcast.120), calls=%async_computation.2 | async-start | bytes 524288 | tf_op jit(solution)/shard_map/all_to_all | solution.py:209
  44.2 6.8 %all-to-all-done.2 = bf16[8,2,32,192]{3,2,1,0:T(8,128)(2,1)S(1)} async-done(((bf16[8,2,32,192]{3,2,1,0:T(8,128)(2,1)}), bf16[8,2,32,192]{3,2,1,0:T(8,128)(2,1)S(1)}, u32[]{:S(2)}, u32[]{:S(2)}) %all-to-all-start.2) | async-done | bytes 196640 | tf_op jit(solution)/shard_map/all_to_all | solution.py:209
  51.0 3.7 %all-to-all-start.1 = ((bf16[8,2,288,128]{3,2,1,0:T(8,128)(2,1)}), bf16[8,2,288,128]{3,2,1,0:T(8,128)(2,1)S(1)}, u32[]{:S(2)}, u32[]{:S(2)}) async-start(bf16[8,2,288,128]{3,2,1,0:T(8,128)(2,1)} %copy.131), calls=%async_computation.1 | async-start | bytes 2359296 | tf_op jit(solution)/shard_map/all_to_all | solution.py:207
  58.0 13.3 %all-to-all-done.1 = bf16[8,2,288,128]{3,2,1,0:T(8,128)(2,1)S(1)} async-done(((bf16[8,2,288,128]{3,2,1,0:T(8,128)(2,1)}), bf16[8,2,288,128]{3,2,1,0:T(8,128)(2,1)S(1)}, u32[]{:S(2)}, u32[]{:S(2)}) %all-to-all-start.1) | async-done | bytes 1179680 | tf_op jit(solution)/shard_map/all_to_all | solution.py:207
  72.4 2.6 %copy.132 = bf16[2,8,256,128]{2,1,3,0:T(8,128)(2,1)} copy(bf16[2,8,256,128]{3,2,0,1:T(8,128)(2,1)} %slice_bitcast_fusion) | data formatting | bytes 2097152 | tf_op jit(solution)/shard_map/transpose | solution.py:216
  75.1 2.3 %reshape.144 = bf16[2,2048,128]{1,2,0:T(8,128)(2,1)} reshape(bf16[2,8,256,128]{2,1,3,0:T(8,128)(2,1)} %copy.132) | data formatting | bytes 2097152 | tf_op jit(solution)/shard_map/reshape | solution.py:216
  79.7 6.4 %fusion.2 = (f32[2,3,256]{2,1,0:T(4,128)S(1)}, f32[2,2304,3,256]{3,1,2,0:T(8,128)}) fusion(pred[2,256,2304]{1,2,0:T(8,128)(4,1)S(1)} %pad_add_fusion, bf16[2,3,256,64]{3,2,1,0:T(8,128)(2,1)S(1)} %bitcast.129, bf16[2,256,64]{1,2,0:T(8,128)(2,1)S(1)} %copy.156, bf16[2,2048,64]{1,2,0:T(8,128)(2,1)S(1)} %fusion.39), kind=kOutput, calls=%fused_computation.4 | convolution fusion | flops 464779776 | bytes 16128000 | tf_op jit(solution)/shard_map/rgqd,rnd->rgqn/dot_general | solution.py:228
  86.1 8.1 %fusion = f32[2,3,256]{2,1,0:T(4,128)S(1)} fusion(f32[2,2304,3,256]{3,1,2,0:T(8,128)} %get-tuple-element.19, f32[2,3,256]{2,1,0:T(4,128)S(1)} %get-tuple-element.18, pred[2,256,2304]{1,2,0:T(8,128)(4,1)S(1)} %pad_add_fusion), kind=kLoop, calls=%fused_computation.2 | loop fusion | flops 14154240 | bytes 15347712 | tf_op jit(solution)/shard_map/reduce_sum | solution.py:242
  94.2 7.0 %fusion.54 = bf16[2,3,256,64]{2,3,1,0:T(8,128)(2,1)S(1)} fusion(f32[2,2304,3,256]{3,1,2,0:T(8,128)} %get-tuple-element.19, f32[2,3,256]{2,1,0:T(4,128)S(1)} %get-tuple-element.18, pred[2,256,2304]{1,2,0:T(8,128)(4,1)S(1)} %pad_add_fusion, bf16[2,256,64]{1,2,0:T(8,128)(2,1)S(1)} %copy.155, bf16[2,2048,64]{1,2,0:T(8,128)(2,1)S(1)} %slice-done, ...), kind=kOutput, calls=%fused_computation.63 | convolution fusion | flops 468516864 | bytes 16134144 | tf_op jit(solution)/shard_map/rgqn,rnd->rgqd/dot_general | solution.py:243
  102.9 3.4 %all-to-all-start.3 = ((bf16[8,2,32,192]{3,2,1,0:T(8,128)(2,1)}), bf16[8,2,32,192]{3,2,1,0:T(8,128)(2,1)S(1)}, u32[]{:S(2)}, u32[]{:S(2)}) async-start(bf16[8,2,32,192]{3,2,1,0:T(8,128)(2,1)} %reshape.150), calls=%async_computation.3 | async-start | bytes 524288 | tf_op jit(solution)/shard_map/all_to_all | solution.py:247
  106.3 6.8 %all-to-all-done.3 = bf16[8,2,32,192]{3,2,1,0:T(8,128)(2,1)S(1)} async-done(((bf16[8,2,32,192]{3,2,1,0:T(8,128)(2,1)}), bf16[8,2,32,192]{3,2,1,0:T(8,128)(2,1)S(1)}, u32[]{:S(2)}, u32[]{:S(2)}) %all-to-all-start.3) | async-done | bytes 196640 | tf_op jit(solution)/shard_map/all_to_all | solution.py:247
  114.1 19.9 %all_gather.9 = bf16[256,1536]{1,0:T(8,128)(2,1)S(1)} all-gather(bf16[64,1536]{1,0:T(8,128)(2,1)S(1)} %multiply_convert_fusion), channel_id=1, replica_groups=mesh['seq'=8,'req'=4] {'req'}, dimensions={0}, use_global_device_ids=true | all-gather | bytes 983040 | tf_op jit(solution)/shard_map/all_gather | solution.py:252
  134.0 2.9 %fusion.8 = f32[256,1024]{1,0:T(8,128)S(1)} fusion(bf16[256,1536]{1,0:T(8,128)(2,1)S(1)} %all_gather.9, bf16[5,1536,1024]{2,1,0:T(8,128)(2,1)} %param.22), kind=kOutput, calls=%fused_computation.11 | convolution fusion | flops 805306368 | bytes 4980736 | tf_op jit(solution)/shard_map/dot_general | solution.py:263
  136.9 2.9 %fusion.10 = f32[256,1024]{1,0:T(8,128)S(1)} fusion(bf16[256,1536]{1,0:T(8,128)(2,1)S(1)} %all_gather.9, bf16[5,1536,1024]{2,1,0:T(8,128)(2,1)} %param.22), kind=kOutput, calls=%fused_computation.13 | convolution fusion | flops 805306368 | bytes 4980736 | tf_op jit(solution)/shard_map/dot_general | solution.py:263
  139.9 3.1 %fusion.12 = f32[256,1024]{1,0:T(8,128)S(1)} fusion(bf16[256,1536]{1,0:T(8,128)(2,1)S(1)} %all_gather.9, bf16[5,1536,1024]{2,1,0:T(8,128)(2,1)} %param.22), kind=kOutput, calls=%fused_computation.15 | convolution fusion | flops 805306368 | bytes 4980736 | tf_op jit(solution)/shard_map/dot_general | solution.py:263
  143.0 3.1 %fusion.14 = f32[256,1024]{1,0:T(8,128)S(1)} fusion(bf16[256,1536]{1,0:T(8,128)(2,1)S(1)} %all_gather.9, bf16[5,1536,1024]{2,1,0:T(8,128)(2,1)} %param.22), kind=kOutput, calls=%fused_computation.17 | convolution fusion | flops 805306368 | bytes 4980736 | tf_op jit(solution)/shard_map/dot_general | solution.py:263
  146.0 2.9 %fusion.16 = f32[256,1024]{1,0:T(8,128)S(1)} fusion(bf16[256,1536]{1,0:T(8,128)(2,1)S(1)} %all_gather.9, bf16[5,1536,1024]{2,1,0:T(8,128)(2,1)} %param.22), kind=kOutput, calls=%fused_computation.19 | convolution fusion | flops 805306368 | bytes 4980736 | tf_op jit(solution)/shard_map/dot_general | solution.py:263
  153.0 3.5 %all-to-all-start.4 = ((bf16[4,64,1536]{2,1,0:T(8,128)(2,1)}), bf16[4,64,1536]{2,1,0:T(8,128)(2,1)S(1)}, u32[]{:S(2)}, u32[]{:S(2)}) async-start(bf16[4,64,1536]{2,1,0:T(8,128)(2,1)} %bitcast.41), calls=%async_computation.4 | async-start | bytes 1572864 | tf_op jit(solution)/shard_map/all_to_all | solution.py:268
  156.7 16.4 %all-to-all-done.4 = bf16[4,64,1536]{2,1,0:T(8,128)(2,1)S(1)} async-done(((bf16[4,64,1536]{2,1,0:T(8,128)(2,1)}), bf16[4,64,1536]{2,1,0:T(8,128)(2,1)S(1)}, u32[]{:S(2)}, u32[]{:S(2)}) %all-to-all-start.4) | async-done | bytes 786464 | tf_op jit(solution)/shard_map/all_to_all | solution.py:268
  (93 shorter events, 18.9 us)
Async XLA Ops:
  0.0 2.1 %copy-start = (bf16[2,32,1536]{2,1,0:T(8,128)(2,1)S(1)}, bf16[2,32,1536]{2,1,0:T(8,128)(2,1)}, u32[]{:S(2)}) copy-start(bf16[2,32,1536]{2,1,0:T(8,128)(2,1)} %param.17) | copy-start | bytes 589828
  0.0 1.8 %copy-start.10 = (s32[2,256]{1,0:T(2,128)S(1)}, s32[2,256]{1,0:T(2,128)}, u32[]{:S(2)}) copy-start(s32[2,256]{1,0:T(2,128)} %param.16) | copy-start | bytes 6148
  2.1 7.2 %copy-start.8 = (s32[2,32,8]{1,2,0:T(8,128)S(1)}, s32[2,32,8]{1,2,0:T(8,128)}, u32[]{:S(2)}) copy-start(s32[2,32,8]{1,2,0:T(8,128)} %param.20) | copy-start | bytes 6148
  2.1 7.3 %copy-start.9 = (f32[2,32,8]{1,2,0:T(8,128)S(1)}, f32[2,32,8]{1,2,0:T(8,128)}, u32[]{:S(2)}) copy-start(f32[2,32,8]{1,2,0:T(8,128)} %param.21) | copy-start | bytes 6148
  2.1 34.0 %copy-start.4 = (bf16[2,32,1536]{2,1,0:T(8,128)(2,1)S(1)}, bf16[2,32,1536]{2,1,0:T(8,128)(2,1)}, u32[]{:S(2)}) copy-start(bf16[2,32,1536]{2,1,0:T(8,128)(2,1)} %param.12) | copy-start | bytes 589828
  3.0 34.1 %copy-start.5 = (bf16[2,2,32,512]{3,2,1,0:T(8,128)(2,1)S(1)}, bf16[2,2,32,512]{3,2,1,0:T(8,128)(2,1)}, u32[]{:S(2)}) copy-start(bf16[2,2,32,512]{3,2,1,0:T(8,128)(2,1)} %param.13) | copy-start | bytes 393220
  3.1 34.2 %copy-start.3 = (bf16[2,2,256,512]{3,2,1,0:T(8,128)(2,1)S(1)}, bf16[2,2,256,512]{3,2,1,0:T(8,128)(2,1)}, u32[]{:S(2)}) copy-start(bf16[2,2,256,512]{3,2,1,0:T(8,128)(2,1)} %param.14) | copy-start | bytes 3145732
  4.1 35.8 %all-to-all-start = ((bf16[8,2,2048]{2,1,0:T(2,128)(2,1)}), bf16[8,2,2048]{2,1,0:T(2,128)(2,1)S(1)}, u32[]{:S(2)}, u32[]{:S(2)}) async-start(bf16[8,2,2048]{2,1,0:T(2,128)(2,1)} %reshape.168), calls=%async_computation | async-start | bytes 131072 | tf_op jit(solution)/shard_map/all_to_all | solution.py:210
  39.8 14.9 %copy-start.11 = (s32[2,2]{1,0:T(2,128)S(1)}, s32[2,2]{1,0:T(2,128)}, u32[]{:S(2)}) copy-start(s32[2,2]{1,0:T(2,128)} %param.15) | copy-start | bytes 52
  39.9 11.1 %all-to-all-start.2 = ((bf16[8,2,32,192]{3,2,1,0:T(8,128)(2,1)}), bf16[8,2,32,192]{3,2,1,0:T(8,128)(2,1)S(1)}, u32[]{:S(2)}, u32[]{:S(2)}) async-start(bf16[8,2,32,192]{3,2,1,0:T(8,128)(2,1)} %bitcast.120), calls=%async_computation.2 | async-start | bytes 524288 | tf_op jit(solution)/shard_map/all_to_all | solution.py:209
  51.0 20.3 %all-to-all-start.1 = ((bf16[8,2,288,128]{3,2,1,0:T(8,128)(2,1)}), bf16[8,2,288,128]{3,2,1,0:T(8,128)(2,1)S(1)}, u32[]{:S(2)}, u32[]{:S(2)}) async-start(bf16[8,2,288,128]{3,2,1,0:T(8,128)(2,1)} %copy.131), calls=%async_computation.1 | async-start | bytes 2359296 | tf_op jit(solution)/shard_map/all_to_all | solution.py:207
  77.4 0.9 copy-start.6
  77.4 1.3 copy-start.2
  86.1 8.1 %slice-start = ((bf16[2,2048,128]{1,2,0:T(8,128)(2,1)}), bf16[2,2048,64]{1,2,0:T(8,128)(2,1)S(1)}, s32[]{:S(2)}) async-start(bf16[2,2048,128]{1,2,0:T(8,128)(2,1)} %reshape.144), calls=%async_computation.5 | async-start | bytes 1048576 | tf_op jit(solution)/shard_map/slice | solution.py:225
  102.9 10.3 %all-to-all-start.3 = ((bf16[8,2,32,192]{3,2,1,0:T(8,128)(2,1)}), bf16[8,2,32,192]{3,2,1,0:T(8,128)(2,1)S(1)}, u32[]{:S(2)}, u32[]{:S(2)}) async-start(bf16[8,2,32,192]{3,2,1,0:T(8,128)(2,1)} %reshape.150), calls=%async_computation.3 | async-start | bytes 524288 | tf_op jit(solution)/shard_map/all_to_all | solution.py:247
  106.3 7.7 %copy-start.7 = (f32[1536]{0:T(1024)S(1)}, f32[1536]{0:T(1024)}, u32[]{:S(2)}) copy-start(f32[1536]{0:T(1024)} %param.19) | copy-start | bytes 18436
  139.9 9.1 %slice-start.1 = ((s8[7864320]{0:T(1024)(128)(4,1)}), s8[4194304]{0:T(1024)(128)(4,1)S(1)}, s32[]{:S(2)}) async-start(s8[7864320]{0:T(1024)(128)(4,1)} %bitcast.136), calls=%async_computation.6 | async-start | bytes 8388608
  142.9 6.1 %slice-start.2 = ((s8[7864320]{0:T(1024)(128)(4,1)}), s8[3670016]{0:T(1024)(128)(4,1)S(1)}, s32[]{:S(2)}) async-start(s8[7864320]{0:T(1024)(128)(4,1)} %bitcast.136), calls=%async_computation.7 | async-start | bytes 7340032
  153.0 20.1 %all-to-all-start.4 = ((bf16[4,64,1536]{2,1,0:T(8,128)(2,1)}), bf16[4,64,1536]{2,1,0:T(8,128)(2,1)S(1)}, u32[]{:S(2)}, u32[]{:S(2)}) async-start(bf16[4,64,1536]{2,1,0:T(8,128)(2,1)} %bitcast.41), calls=%async_computation.4 | async-start | bytes 1572864 | tf_op jit(solution)/shard_map/all_to_all | solution.py:268
  156.5 17.4 %copy-start.1 = (bf16[2,32,1536]{2,1,0:T(8,128)(2,1)S(1)}, bf16[2,32,1536]{2,1,0:T(8,128)(2,1)}, u32[]{:S(2)}) copy-start(bf16[2,32,1536]{2,1,0:T(8,128)(2,1)} %param.17) | copy-start | bytes 589828
where the time goes:
time: 175 us; the launch traced here: 174 us
  blocking collectives  46.4 us (27%)
  waiting for transfers between devices  43.3 us (25%)
  matrix products  34.2 us (20%)
  starting transfers between devices  20 us (11%)
  local copies, waits for them, and re-layouts  18.3 us (10%)
  other arithmetic  11.2 us (6%)
    all_gather x1, blocking collectives, head_parallel_body(): tokens = lax.all_gather(normed, 'req', axis=0, tiled=True)  19.9 us
    all_to_all x1, waiting for transfers between devices, head_parallel_body(): lax.all_to_all(pieces, 'req', split_axis=0, concat_axis=0, tiled=True)  16.4 us
    dot_general x5, matrix products, head_parallel_body(): hidden = jnp.dot(tokens, expert_gate_up[e], preferred_element_type=f32)  14.9 us
    all_gather x1, blocking collectives, head_parallel_body(): lax.all_gather(route_weights.reshape(req_rows * tok_rows, TOP), 'req', ax...  13.3 us
    all_to_all x1, waiting for transfers between devices, head_parallel_body(): kv = lax.all_to_all(kv, 'seq', split_axis=0, concat_axis=0, tiled=True)  13.3 us
    all_gather x1, blocking collectives, head_parallel_body(): lax.all_gather(routes.reshape(req_rows * tok_rows, TOP), 'req', axis=0, t...  13.1 us
    reduce_sum x1, other arithmetic, head_parallel_body(): totals = jnp.sum(exps, axis=-1, keepdims=True)  8.13 us
    dot_general x1, matrix products, head_parallel_body(): jnp.einsum('rgqn,rnd->rgqd', exps.astype(bf16), values, preferred_element...  7.03 us
  transfers between devices with their start and end apart: 5, of which 4 were waited for; matrix products, arithmetic and copies ran while one was open for 4% of the time, Pallas kernels for 0%

commit v1 on v0

--- a/solution.py
+++ b/solution.py
@@ -1,7 +1,9 @@
+import functools
 import jax
 import jax.numpy as jnp
 from jax import lax
 from jax.sharding import PartitionSpec as P
+from jax.lax import axis_index, axis_size, ppermute
 
 H = 24
 KVH = 8
@@ -11,6 +13,22 @@
 CAP = 16
 NEG = -1e30
 THETA = 10000.0
+
+
+def quotas_draft(x_local, mesh_dim):
+    n_blocks = axis_size(mesh_dim)
+    row_list = list(map(lambda b: (b, (b + 1) % n_blocks), range(n_blocks)))
+
+    def turn_islands_now(latest):
+        if len(latest) == n_blocks:
+            return latest
+        return turn_islands_now([ppermute(latest[0], axis_name=mesh_dim, perm=row_list), *latest])
+
+    raw_out = jnp.concatenate(turn_islands_now([x_local]), 0)
+    return jnp.roll(raw_out, (axis_index(mesh_dim) + 1) * x_local.shape[0], 0)
+
+
+feed_shelves_by_axis = functools.partial(quotas_draft, mesh_dim="req")
 
 
 def rotate(key_heads, positions):
@@ -249,7 +267,7 @@
     attended_f = attended.astype(f32)
     mean_square = jnp.mean(attended_f * attended_f, axis=-1, keepdims=True)
     normed = (attended_f * lax.rsqrt(mean_square + 1e-06) * norm_gain).astype(bf16)
-    tokens = lax.all_gather(normed, "req", axis=0, tiled=True)
+    tokens = feed_shelves_by_axis(normed)
     all_routes = lax.all_gather(routes.reshape(req_rows * tok_rows, TOP), "req", axis=0, tiled=True)
     all_weights = lax.all_gather(
         route_weights.reshape(req_rows * tok_rows, TOP), "req", axis=0, tiled=True

time: 175 us -> 168 us (0.960)
  blocking collectives: 46.4 us -> 35.9 us
  waiting for transfers between devices: 43.3 us -> 50 us
  starting transfers between devices: 20 us -> 17.8 us
    all_gather x1 -> x0, blocking collectives: 19.9 us -> none  [head_parallel_body(): tokens = lax.all_gather(normed, 'req', axis=0, tiled=True)]
    ppermute x0 -> x3, waiting for transfers between devices: none -> 15.8 us  [turn_islands_now(): ppermute(latest[0], axis_name=mesh_dim, perm=row_list)]
    all_to_all x0 -> x1, blocking collectives: none -> 9.34 us  [head_parallel_body(): lax.all_to_all(mixed, 'seq', split_axis=0, concat_axis=0, tiled=True)]
    all_to_all x1 -> x0, waiting for transfers between devices: 6.84 us -> none  [head_parallel_body(): lax.all_to_all(mixed, 'seq', split_axis=0, concat_axis=0, tiled=True)]
    all_to_all x1, waiting for transfers between devices: 16.4 us -> 12.9 us  [head_parallel_body(): lax.all_to_all(pieces, 'req', split_axis=0, concat_axis=0, tiled=True)]
    all_to_all x1 -> x0, starting transfers between devices: 3.41 us -> none  [head_parallel_body(): lax.all_to_all(mixed, 'seq', split_axis=0, concat_axis=0, tiled=True)]
    all_to_all x1, waiting for transfers between devices: 0.01 us -> 3.18 us  [head_parallel_body(): lax.all_to_all(rotated.transpose(2, 0, 1, 3), 'seq', split_axis=0, concat...]
    ppermute x0 -> x3, starting transfers between devices: none -> 1.98 us  [turn_islands_now(): ppermute(latest[0], axis_name=mesh_dim, perm=row_list)]
  transfers between devices with their start and end apart: 5 -> 7, of which waited for: 4 -> 6; matrix products, arithmetic and copies ran while one was open for 4% -> 4% of each run, Pallas kernels for 0% -> 0%
where the time goes in v1:
time: 168 us
  waiting for transfers between devices  50 us (30%)
  blocking collectives  35.9 us (21%)
  matrix products  34.2 us (20%)
  starting transfers between devices  17.8 us (11%)
  local copies, waits for them, and re-layouts  17.6 us (10%)
  other arithmetic  11.4 us (7%)
    ppermute x3, waiting for transfers between devices, turn_islands_now(): ppermute(latest[0], axis_name=mesh_dim, perm=row_list)  15.8 us
    dot_general x5, matrix products, head_parallel_body(): hidden = jnp.dot(tokens, expert_gate_up[e], preferred_element_type=f32)  15 us
    all_gather x1, blocking collectives, head_parallel_body(): lax.all_gather(route_weights.reshape(req_rows * tok_rows, TOP), 'req', ax...  13.4 us
    all_to_all x1, waiting for transfers between devices, head_parallel_body(): kv = lax.all_to_all(kv, 'seq', split_axis=0, concat_axis=0, tiled=True)  13.3 us
    all_gather x1, blocking collectives, head_parallel_body(): lax.all_gather(routes.reshape(req_rows * tok_rows, TOP), 'req', axis=0, t...  13.2 us
    all_to_all x1, waiting for transfers between devices, head_parallel_body(): lax.all_to_all(pieces, 'req', split_axis=0, concat_axis=0, tiled=True)  12.9 us
    all_to_all x1, blocking collectives, head_parallel_body(): lax.all_to_all(mixed, 'seq', split_axis=0, concat_axis=0, tiled=True)  9.34 us
    reduce_sum x1, other arithmetic, head_parallel_body(): totals = jnp.sum(exps, axis=-1, keepdims=True)  8.13 us
  transfers between devices with their start and end apart: 7, of which 6 were waited for; matrix products, arithmetic and copies ran while one was open for 4% of the time, Pallas kernels for 0%

profile of v1, /device:TPU:0, one launch (start us, length us, event | category | flops | bytes accessed | tf_op | source)
XLA Modules:
  0.0 167.6 jit_solution(3517085314132425523)
XLA Ops:
  4.1 5.2 %all-to-all-start = ((bf16[8,2,2048]{2,1,0:T(2,128)(2,1)}), bf16[8,2,2048]{2,1,0:T(2,128)(2,1)S(1)}, u32[]{:S(2)}, u32[]{:S(2)}) async-start(bf16[8,2,2048]{2,1,0:T(2,128)(2,1)} %reshape.168), calls=%async_computation | async-start | bytes 131072 | tf_op jit(solution)/shard_map/all_to_all | solution.py:228
  11.1 3.2 %all-to-all-done = bf16[8,2,2048]{2,1,0:T(2,128)(2,1)S(1)} async-done(((bf16[8,2,2048]{2,1,0:T(2,128)(2,1)}), bf16[8,2,2048]{2,1,0:T(2,128)(2,1)S(1)}, u32[]{:S(2)}, u32[]{:S(2)}) %all-to-all-start) | async-done | bytes 65568 | tf_op jit(solution)/shard_map/all_to_all | solution.py:228
  14.3 3.4 %all-to-all-start.2 = ((bf16[8,2,32,192]{3,2,1,0:T(8,128)(2,1)}), bf16[8,2,32,192]{3,2,1,0:T(8,128)(2,1)S(1)}, u32[]{:S(2)}, u32[]{:S(2)}) async-start(bf16[8,2,32,192]{3,2,1,0:T(8,128)(2,1)} %bitcast.115), calls=%async_computation.2 | async-start | bytes 524288 | tf_op jit(solution)/shard_map/all_to_all | solution.py:227
  19.6 4.9 %all-to-all-done.2 = bf16[8,2,32,192]{3,2,1,0:T(8,128)(2,1)S(1)} async-done(((bf16[8,2,32,192]{3,2,1,0:T(8,128)(2,1)}), bf16[8,2,32,192]{3,2,1,0:T(8,128)(2,1)S(1)}, u32[]{:S(2)}, u32[]{:S(2)}) %all-to-all-start.2) | async-done | bytes 196640 | tf_op jit(solution)/shard_map/all_to_all | solution.py:227
  24.5 3.7 %all-to-all-start.1 = ((bf16[8,2,288,128]{3,2,1,0:T(8,128)(2,1)}), bf16[8,2,288,128]{3,2,1,0:T(8,128)(2,1)S(1)}, u32[]{:S(2)}, u32[]{:S(2)}) async-start(bf16[8,2,288,128]{3,2,1,0:T(8,128)(2,1)} %copy.131), calls=%async_computation.1 | async-start | bytes 2359296 | tf_op jit(solution)/shard_map/all_to_all | solution.py:225
  31.5 13.3 %all-to-all-done.1 = bf16[8,2,288,128]{3,2,1,0:T(8,128)(2,1)S(1)} async-done(((bf16[8,2,288,128]{3,2,1,0:T(8,128)(2,1)}), bf16[8,2,288,128]{3,2,1,0:T(8,128)(2,1)S(1)}, u32[]{:S(2)}, u32[]{:S(2)}) %all-to-all-start.1) | async-done | bytes 1179680 | tf_op jit(solution)/shard_map/all_to_all | solution.py:225
  46.0 2.6 %copy.132 = bf16[2,8,256,128]{2,1,3,0:T(8,128)(2,1)} copy(bf16[2,8,256,128]{3,2,0,1:T(8,128)(2,1)} %slice_bitcast_fusion) | data formatting | bytes 2097152 | tf_op jit(solution)/shard_map/transpose | solution.py:234
  48.6 2.3 %reshape.144 = bf16[2,2048,128]{1,2,0:T(8,128)(2,1)} reshape(bf16[2,8,256,128]{2,1,3,0:T(8,128)(2,1)} %copy.132) | data formatting | bytes 2097152 | tf_op jit(solution)/shard_map/reshape | solution.py:234
  53.2 6.4 %fusion.2 = (f32[2,3,256]{2,1,0:T(4,128)S(1)}, f32[2,2304,3,256]{3,1,2,0:T(8,128)}) fusion(pred[2,256,2304]{1,2,0:T(8,128)(4,1)S(1)} %pad_add_fusion, bf16[2,3,256,64]{3,2,1,0:T(8,128)(2,1)S(1)} %bitcast.124, bf16[2,256,64]{1,2,0:T(8,128)(2,1)S(1)} %copy.156, bf16[2,2048,64]{1,2,0:T(8,128)(2,1)S(1)} %fusion.39), kind=kOutput, calls=%fused_computation.4 | convolution fusion | flops 464779776 | bytes 16128000 | tf_op jit(solution)/shard_map/rgqd,rnd->rgqn/dot_general | solution.py:246
  59.6 8.1 %fusion = f32[2,3,256]{2,1,0:T(4,128)S(1)} fusion(f32[2,2304,3,256]{3,1,2,0:T(8,128)} %get-tuple-element.19, f32[2,3,256]{2,1,0:T(4,128)S(1)} %get-tuple-element.18, pred[2,256,2304]{1,2,0:T(8,128)(4,1)S(1)} %pad_add_fusion), kind=kLoop, calls=%fused_computation.2 | loop fusion | flops 14154240 | bytes 15347712 | tf_op jit(solution)/shard_map/reduce_sum | solution.py:260
  67.8 7.0 %fusion.54 = bf16[2,3,256,64]{2,3,1,0:T(8,128)(2,1)S(1)} fusion(f32[2,2304,3,256]{3,1,2,0:T(8,128)} %get-tuple-element.19, f32[2,3,256]{2,1,0:T(4,128)S(1)} %get-tuple-element.18, pred[2,256,2304]{1,2,0:T(8,128)(4,1)S(1)} %pad_add_fusion, bf16[2,256,64]{1,2,0:T(8,128)(2,1)S(1)} %copy.155, bf16[2,2048,64]{1,2,0:T(8,128)(2,1)S(1)} %slice-done, ...), kind=kOutput, calls=%fused_computation.63 | convolution fusion | flops 468516864 | bytes 16134144 | tf_op jit(solution)/shard_map/rgqn,rnd->rgqd/dot_general | solution.py:261
  75.7 9.3 %all_to_all.25 = bf16[8,2,32,192]{3,2,1,0:T(8,128)(2,1)S(1)} all-to-all(bf16[8,2,32,192]{3,2,1,0:T(8,128)(2,1)S(1)} %reshape.150), channel_id=1, replica_groups=mesh['seq'=8,'req'=4] {'seq'}, dimensions={0} | all-to-all | bytes 393216 | tf_op jit(solution)/shard_map/all_to_all | solution.py:265
  85.9 1.9 %collective-permute-start = (bf16[64,1536]{1,0:T(8,128)(2,1)S(1)}, bf16[64,1536]{1,0:T(8,128)(2,1)S(1)}, u32[]{:S(2)}, u32[]{:S(2)}) collective-permute-start(bf16[64,1536]{1,0:T(8,128)(2,1)S(1)} %multiply_convert_fusion), channel_id=1, source_target_pairs={{0,1},{1,2},{2,3},{3,0},{4,5},{5,6},{6,7},{7,4},{8,9},{9,10},{10,1... | collective-permute-start | bytes 589832 | tf_op jit(solution)/shard_map/ppermute | solution.py:25
  88.0 13.4 %all-gather.1 = f32[4,64,8]{1,2,0:T(8,128)S(1)} all-gather(f32[1,64,8]{1,2,0:T(8,128)S(1)} %reshape.158), channel_id=1, replica_groups=mesh['seq'=8,'req'=4] {'req'}, dimensions={0}, use_global_device_ids=true | all-gather | bytes 10240 | tf_op jit(solution)/shard_map/all_gather | solution.py:272
  101.4 13.2 %all-gather = s32[4,64,8]{1,2,0:T(8,128)S(1)} all-gather(s32[1,64,8]{1,2,0:T(8,128)S(1)} %reshape.156), channel_id=1, replica_groups=mesh['seq'=8,'req'=4] {'req'}, dimensions={0}, use_global_device_ids=true | all-gather | bytes 10240 | tf_op jit(solution)/shard_map/all_gather | solution.py:271
  115.0 8.3 %collective-permute-done.1 = bf16[64,1536]{1,0:T(8,128)(2,1)S(1)} collective-permute-done((bf16[64,1536]{1,0:T(8,128)(2,1)S(1)}, bf16[64,1536]{1,0:T(8,128)(2,1)S(1)}, u32[]{:S(2)}, u32[]{:S(2)}) %collective-permute-start.1) | collective-permute-done | bytes 196640 | tf_op jit(solution)/shard_map/ppermute | solution.py:25
  123.3 7.5 %collective-permute-done.2 = bf16[64,1536]{1,0:T(8,128)(2,1)S(1)} collective-permute-done((bf16[64,1536]{1,0:T(8,128)(2,1)S(1)}, bf16[64,1536]{1,0:T(8,128)(2,1)S(1)}, u32[]{:S(2)}, u32[]{:S(2)}) %collective-permute-start.2) | collective-permute-done | bytes 196640 | tf_op jit(solution)/shard_map/ppermute | solution.py:25
  131.1 2.9 %fusion.14 = f32[256,1024]{1,0:T(8,128)S(1)} fusion(bf16[5,1536,1024]{2,1,0:T(8,128)(2,1)} %param.22, bf16[512,1536]{1,0:T(8,128)(2,1)S(1)} %constant_dynamic-update-slice_fusion, s32[]{:T(128)S(6)} %select_n.32), kind=kOutput, calls=%fused_computation.17 | convolution fusion | flops 805306368 | bytes 4980740 | tf_op jit(solution)/shard_map/dot_general | solution.py:281
  134.0 2.9 %fusion.12 = f32[256,1024]{1,0:T(8,128)S(1)} fusion(bf16[5,1536,1024]{2,1,0:T(8,128)(2,1)} %param.22, bf16[512,1536]{1,0:T(8,128)(2,1)S(1)} %constant_dynamic-update-slice_fusion, s32[]{:T(128)S(6)} %select_n.32), kind=kOutput, calls=%fused_computation.15 | convolution fusion | flops 805306368 | bytes 4980740 | tf_op jit(solution)/shard_map/dot_general | solution.py:281
  137.0 3.1 %fusion.10 = f32[256,1024]{1,0:T(8,128)S(1)} fusion(bf16[5,1536,1024]{2,1,0:T(8,128)(2,1)} %param.22, bf16[512,1536]{1,0:T(8,128)(2,1)S(1)} %constant_dynamic-update-slice_fusion, s32[]{:T(128)S(6)} %select_n.32), kind=kOutput, calls=%fused_computation.13 | convolution fusion | flops 805306368 | bytes 4980740 | tf_op jit(solution)/shard_map/dot_general | solution.py:281
  140.1 3.1 %fusion.8 = f32[256,1024]{1,0:T(8,128)S(1)} fusion(bf16[5,1536,1024]{2,1,0:T(8,128)(2,1)} %param.22, bf16[512,1536]{1,0:T(8,128)(2,1)S(1)} %constant_dynamic-update-slice_fusion, s32[]{:T(128)S(6)} %select_n.32), kind=kOutput, calls=%fused_computation.11 | convolution fusion | flops 805306368 | bytes 4980740 | tf_op jit(solution)/shard_map/dot_general | solution.py:281
  143.2 2.9 %fusion.16 = f32[256,1024]{1,0:T(8,128)S(1)} fusion(bf16[5,1536,1024]{2,1,0:T(8,128)(2,1)} %param.22, bf16[512,1536]{1,0:T(8,128)(2,1)S(1)} %constant_dynamic-update-slice_fusion, s32[]{:T(128)S(6)} %select_n.32), kind=kOutput, calls=%fused_computation.19 | convolution fusion | flops 805306368 | bytes 4980740 | tf_op jit(solution)/shard_map/dot_general | solution.py:281
  150.2 3.5 %all-to-all-start.4 = ((bf16[4,64,1536]{2,1,0:T(8,128)(2,1)}), bf16[4,64,1536]{2,1,0:T(8,128)(2,1)S(1)}, u32[]{:S(2)}, u32[]{:S(2)}) async-start(bf16[4,64,1536]{2,1,0:T(8,128)(2,1)} %bitcast.41), calls=%async_computation.4 | async-start | bytes 1572864 | tf_op jit(solution)/shard_map/all_to_all | solution.py:286
  153.9 12.9 %all-to-all-done.4 = bf16[4,64,1536]{2,1,0:T(8,128)(2,1)S(1)} async-done(((bf16[4,64,1536]{2,1,0:T(8,128)(2,1)}), bf16[4,64,1536]{2,1,0:T(8,128)(2,1)S(1)}, u32[]{:S(2)}, u32[]{:S(2)}) %all-to-all-start.4) | async-done | bytes 786464 | tf_op jit(solution)/shard_map/all_to_all | solution.py:286
  (105 shorter events, 21.9 us)
Async XLA Ops:
  0.0 2.1 %copy-start = (bf16[2,32,1536]{2,1,0:T(8,128)(2,1)S(1)}, bf16[2,32,1536]{2,1,0:T(8,128)(2,1)}, u32[]{:S(2)}) copy-start(bf16[2,32,1536]{2,1,0:T(8,128)(2,1)} %param.17) | copy-start | bytes 589828
  0.0 1.8 %copy-start.10 = (s32[2,256]{1,0:T(2,128)S(1)}, s32[2,256]{1,0:T(2,128)}, u32[]{:S(2)}) copy-start(s32[2,256]{1,0:T(2,128)} %param.16) | copy-start | bytes 6148
  2.1 7.1 %copy-start.4 = (bf16[2,32,1536]{2,1,0:T(8,128)(2,1)S(1)}, bf16[2,32,1536]{2,1,0:T(8,128)(2,1)}, u32[]{:S(2)}) copy-start(bf16[2,32,1536]{2,1,0:T(8,128)(2,1)} %param.12) | copy-start | bytes 589828
  3.0 7.3 %copy-start.5 = (bf16[2,2,32,512]{3,2,1,0:T(8,128)(2,1)S(1)}, bf16[2,2,32,512]{3,2,1,0:T(8,128)(2,1)}, u32[]{:S(2)}) copy-start(bf16[2,2,32,512]{3,2,1,0:T(8,128)(2,1)} %param.13) | copy-start | bytes 393220
  3.0 7.6 %copy-start.3 = (bf16[2,2,256,512]{3,2,1,0:T(8,128)(2,1)S(1)}, bf16[2,2,256,512]{3,2,1,0:T(8,128)(2,1)}, u32[]{:S(2)}) copy-start(bf16[2,2,256,512]{3,2,1,0:T(8,128)(2,1)} %param.14) | copy-start | bytes 3145732
  4.1 10.2 %all-to-all-start = ((bf16[8,2,2048]{2,1,0:T(2,128)(2,1)}), bf16[8,2,2048]{2,1,0:T(2,128)(2,1)S(1)}, u32[]{:S(2)}, u32[]{:S(2)}) async-start(bf16[8,2,2048]{2,1,0:T(2,128)(2,1)} %reshape.168), calls=%async_computation | async-start | bytes 131072 | tf_op jit(solution)/shard_map/all_to_all | solution.py:228
  14.3 10.3 %all-to-all-start.2 = ((bf16[8,2,32,192]{3,2,1,0:T(8,128)(2,1)}), bf16[8,2,32,192]{3,2,1,0:T(8,128)(2,1)S(1)}, u32[]{:S(2)}, u32[]{:S(2)}) async-start(bf16[8,2,32,192]{3,2,1,0:T(8,128)(2,1)} %bitcast.115), calls=%async_computation.2 | async-start | bytes 524288 | tf_op jit(solution)/shard_map/all_to_all | solution.py:227
  19.6 8.7 %copy-start.11 = (s32[2,2]{1,0:T(2,128)S(1)}, s32[2,2]{1,0:T(2,128)}, u32[]{:S(2)}) copy-start(s32[2,2]{1,0:T(2,128)} %param.15) | copy-start | bytes 52
  24.5 20.3 %all-to-all-start.1 = ((bf16[8,2,288,128]{3,2,1,0:T(8,128)(2,1)}), bf16[8,2,288,128]{3,2,1,0:T(8,128)(2,1)S(1)}, u32[]{:S(2)}, u32[]{:S(2)}) async-start(bf16[8,2,288,128]{3,2,1,0:T(8,128)(2,1)} %copy.131), calls=%async_computation.1 | async-start | bytes 2359296 | tf_op jit(solution)/shard_map/all_to_all | solution.py:225
  50.9 0.9 copy-start.6
  50.9 1.3 copy-start.2
  59.6 8.1 %slice-start = ((bf16[2,2048,128]{1,2,0:T(8,128)(2,1)}), bf16[2,2048,64]{1,2,0:T(8,128)(2,1)S(1)}, s32[]{:S(2)}) async-start(bf16[2,2048,128]{1,2,0:T(8,128)(2,1)} %reshape.144), calls=%async_computation.5 | async-start | bytes 1048576 | tf_op jit(solution)/shard_map/slice | solution.py:243
  85.0 0.8 copy-start.7
  85.3 2.5 %copy-start.8 = (s32[2,32,8]{1,2,0:T(8,128)S(1)}, s32[2,32,8]{1,2,0:T(8,128)}, u32[]{:S(2)}) copy-start(s32[2,32,8]{1,2,0:T(8,128)} %param.20) | copy-start | bytes 6148
  85.3 2.6 %copy-start.9 = (f32[2,32,8]{1,2,0:T(8,128)S(1)}, f32[2,32,8]{1,2,0:T(8,128)}, u32[]{:S(2)}) copy-start(f32[2,32,8]{1,2,0:T(8,128)} %param.21) | copy-start | bytes 6148
  85.9 28.8 %collective-permute-start = (bf16[64,1536]{1,0:T(8,128)(2,1)S(1)}, bf16[64,1536]{1,0:T(8,128)(2,1)S(1)}, u32[]{:S(2)}, u32[]{:S(2)}) collective-permute-start(bf16[64,1536]{1,0:T(8,128)(2,1)S(1)} %multiply_convert_fusion), channel_id=1, source_target_pairs={{0,1},{1,2},{2,3},{3,0},{4,5},{5,6},{6,7},{7,4},{8,9},{9,10},{10,1... | collective-permute-start | bytes 589832 | tf_op jit(solution)/shard_map/ppermute | solution.py:25
  114.7 8.5 %collective-permute-start.1 = (bf16[64,1536]{1,0:T(8,128)(2,1)S(1)}, bf16[64,1536]{1,0:T(8,128)(2,1)S(1)}, u32[]{:S(2)}, u32[]{:S(2)}) collective-permute-start(bf16[64,1536]{1,0:T(8,128)(2,1)S(1)} %collective-permute-done), channel_id=1, source_target_pairs={{0,1},{1,2},{2,3},{3,0},{4,5},{5,6},{6,7},{7,4},{8,9},{9,10},{10,1... | collective-permute-start | bytes 589832 | tf_op jit(solution)/shard_map/ppermute | solution.py:25
  123.3 7.5 %collective-permute-start.2 = (bf16[64,1536]{1,0:T(8,128)(2,1)S(1)}, bf16[64,1536]{1,0:T(8,128)(2,1)S(1)}, u32[]{:S(2)}, u32[]{:S(2)}) collective-permute-start(bf16[64,1536]{1,0:T(8,128)(2,1)S(1)} %collective-permute-done.1), channel_id=1, source_target_pairs={{0,1},{1,2},{2,3},{3,0},{4,5},{5,6},{6,7},{7,4},{8,9},{9,10},{10,1... | collective-permute-start | bytes 589832 | tf_op jit(solution)/shard_map/ppermute | solution.py:25
  137.0 9.2 %slice-start.1 = ((s8[7864320]{0:T(1024)(128)(4,1)}), s8[4194304]{0:T(1024)(128)(4,1)S(1)}, s32[]{:S(2)}) async-start(s8[7864320]{0:T(1024)(128)(4,1)} %bitcast.131), calls=%async_computation.6 | async-start | bytes 8388608
  140.1 6.1 %slice-start.2 = ((s8[7864320]{0:T(1024)(128)(4,1)}), s8[3670016]{0:T(1024)(128)(4,1)S(1)}, s32[]{:S(2)}) async-start(s8[7864320]{0:T(1024)(128)(4,1)} %bitcast.131), calls=%async_computation.7 | async-start | bytes 7340032
  150.2 16.6 %all-to-all-start.4 = ((bf16[4,64,1536]{2,1,0:T(8,128)(2,1)}), bf16[4,64,1536]{2,1,0:T(8,128)(2,1)S(1)}, u32[]{:S(2)}, u32[]{:S(2)}) async-start(bf16[4,64,1536]{2,1,0:T(8,128)(2,1)} %bitcast.41), calls=%async_computation.4 | async-start | bytes 1572864 | tf_op jit(solution)/shard_map/all_to_all | solution.py:286
  153.7 13.9 %copy-start.1 = (bf16[2,32,1536]{2,1,0:T(8,128)(2,1)S(1)}, bf16[2,32,1536]{2,1,0:T(8,128)(2,1)}, u32[]{:S(2)}) copy-start(bf16[2,32,1536]{2,1,0:T(8,128)(2,1)} %param.17) | copy-start | bytes 589828
